TPU v7x, 512 devices: a whole 4x8x8 slice. The times are simulated.
512 devices in a mesh: tm: 32 (over y_lo, z), fsdp: 16 (over x, y_hi, core).
Axes of the slice: x: 4, y: 8 (y_hi: 2, y_lo: 4; y = y_hi * 4 + y_lo), z: 8, core: 2. Of those that a mesh axis runs over, the one named last changes fastest.
Arguments:
- queries: bfloat16 [128, 512, 12, 128], P('tm', 'fsdp'), may hold values from -5 to 5
- key_states: bfloat16 [128, 512, 12, 128], P('tm', 'fsdp'), may hold values from -5 to 5
- value_states: bfloat16 [128, 512, 12, 128], P('tm', 'fsdp'), may hold values from -6 to 6
- out_grad: bfloat16 [128, 512, 3072], P('tm', 'fsdp'), may hold values from -6 to 6
- out_proj: bfloat16 [1536, 3072], P('fsdp'), may hold values from -0.109375 to 0.109375
Outputs:
- query_grad: bfloat16 [128, 512, 12, 128], P('tm', 'fsdp')
- key_grad: bfloat16 [128, 512, 12, 128], P('tm', 'fsdp')
- value_grad: bfloat16 [128, 512, 12, 128], P('tm', 'fsdp')
All inputs are finite; a program needn't handle non-finite values.
Results may differ from a plain program's by a relative error of at most 0.03.
Values may be sent and summed in bfloat16 or wider, within the bound.
A program may use at most 64 MiB of HBM per device.

v0:
```python
import jax
import jax.numpy as jnp
from jax import lax
from jax.sharding import PartitionSpec as P


def attend_back(query_block, key_block, value_block, grad_block):
    score_scale = query_block.shape[-1] ** (-0.5)
    scores = (
        jnp.einsum("fphd,gphd->phfg", query_block, key_block, preferred_element_type=jnp.float32)
        * score_scale
    )
    peak = jnp.max(scores, axis=-1, keepdims=True)
    expo = jnp.exp(scores - peak)
    probs = expo / jnp.sum(expo, axis=-1, keepdims=True)
    probs_b = probs.astype(jnp.bfloat16)
    attn_out = jnp.einsum(
        "phfg,gphd->fphd", probs_b, value_block, preferred_element_type=jnp.float32
    )
    row_delta = jnp.einsum("fphd,fphd->phf", grad_block.astype(jnp.float32), attn_out)
    dprobs = jnp.einsum(
        "fphd,gphd->phfg", grad_block, value_block, preferred_element_type=jnp.float32
    )
    dscores = (probs * (dprobs - row_delta[..., None])).astype(jnp.bfloat16)
    query_grad = (
        jnp.einsum("phfg,gphd->fphd", dscores, key_block, preferred_element_type=jnp.float32)
        * score_scale
    ).astype(jnp.bfloat16)
    key_grad = (
        jnp.einsum("phfg,fphd->gphd", dscores, query_block, preferred_element_type=jnp.float32)
        * score_scale
    ).astype(jnp.bfloat16)
    value_grad = jnp.einsum(
        "phfg,fphd->gphd", probs_b, grad_block, preferred_element_type=jnp.float32
    ).astype(jnp.bfloat16)
    return (query_grad, key_grad, value_grad)


def send_back(grads):
    return (
        lax.all_to_all(grads[0], "tm", split_axis=0, concat_axis=1, tiled=True),
        lax.all_to_all(grads[1], "tm", split_axis=0, concat_axis=1, tiled=True),
        lax.all_to_all(grads[2], "tm", split_axis=0, concat_axis=1, tiled=True),
    )


def body(queries, key_states, value_states, out_grad, out_proj):
    frames_dev, pos_dev, heads, head_size = queries.shape
    width = out_grad.shape[-1]
    flat = out_grad.reshape(frames_dev * pos_dev, width)
    grad_flat = lax.dot_general(
        flat,
        lax.all_gather(out_proj, "fsdp", axis=0, tiled=True),
        (((1,), (1,)), ((), ())),
        preferred_element_type=jnp.float32,
    ).astype(jnp.bfloat16)
    grad_attn = grad_flat.reshape(frames_dev, pos_dev, heads, head_size)
    results = send_back(
        attend_back(
            lax.all_to_all(queries, "tm", split_axis=1, concat_axis=0, tiled=True),
            lax.all_to_all(key_states, "tm", split_axis=1, concat_axis=0, tiled=True),
            lax.all_to_all(value_states, "tm", split_axis=1, concat_axis=0, tiled=True),
            lax.all_to_all(grad_attn, "tm", split_axis=1, concat_axis=0, tiled=True),
        )
    )
    return (results[0], results[1], results[2])


def solution(mesh):
    return jax.shard_map(
        body,
        mesh=mesh,
        in_specs=(
            P("tm", "fsdp", None, None),
            P("tm", "fsdp", None, None),
            P("tm", "fsdp", None, None),
            P("tm", "fsdp", None),
            P("fsdp", None),
        ),
        out_specs=(
            P("tm", "fsdp", None, None),
            P("tm", "fsdp", None, None),
            P("tm", "fsdp", None, None),
        ),
        check_vma=False,
    )
```

profile of v0, /device:TPU:1, one launch (start us, length us, event | category | flops | bytes accessed | tf_op | source)
XLA Modules:
  0.0 254.3 jit_solution(9501734445395635205)
XLA Ops:
  7.2 0.0 copy-start
  7.2 0.0 all-gather.2.cloned.1.call-start
  7.2 0.7 all-gather.2.cloned.1.call-update
  7.9 2.0 copy.39
  9.9 14.3 %all-to-all-start = ((bf16[4,32,12,128]{3,2,0,1:T(8,128)(2,1)}), bf16[4,32,12,128]{3,2,0,1:T(8,128)(2,1)S(1)}, u32[]{:S(2)}, u32[]{:S(2)}) async-start(bf16[4,32,12,128]{3,2,0,1:T(8,128)(2,1)} %copy.39), calls=%async_computation | async-start | bytes 1048576 | tf_op jit(solution)/shard_map/all_to_all | solution.py:60
  24.2 2.0 copy.41
  26.2 19.3 %all-to-all-done = bf16[4,32,12,128]{3,2,0,1:T(8,128)(2,1)S(1)} async-done(((bf16[4,32,12,128]{3,2,0,1:T(8,128)(2,1)}), bf16[4,32,12,128]{3,2,0,1:T(8,128)(2,1)S(1)}, u32[]{:S(2)}, u32[]{:S(2)}) %all-to-all-start) | async-done | bytes 393248 | tf_op jit(solution)/shard_map/all_to_all | solution.py:60
  45.5 8.5 %all-to-all-start.1 = ((bf16[4,32,12,128]{3,2,0,1:T(8,128)(2,1)}), bf16[4,32,12,128]{3,2,0,1:T(8,128)(2,1)S(1)}, u32[]{:S(2)}, u32[]{:S(2)}) async-start(bf16[4,32,12,128]{3,2,0,1:T(8,128)(2,1)} %copy.41), calls=%async_computation.1 | async-start | bytes 1048576 | tf_op jit(solution)/shard_map/all_to_all | solution.py:61
  54.0 2.0 copy.45
  56.0 11.8 %all-to-all-done.1 = bf16[4,32,12,128]{3,2,0,1:T(8,128)(2,1)S(1)} async-done(((bf16[4,32,12,128]{3,2,0,1:T(8,128)(2,1)}), bf16[4,32,12,128]{3,2,0,1:T(8,128)(2,1)S(1)}, u32[]{:S(2)}, u32[]{:S(2)}) %all-to-all-start.1) | async-done | bytes 393248 | tf_op jit(solution)/shard_map/all_to_all | solution.py:61
  67.8 8.5 %all-to-all-start.3 = ((bf16[4,32,12,128]{3,2,0,1:T(8,128)(2,1)}), bf16[4,32,12,128]{3,2,0,1:T(8,128)(2,1)S(1)}, u32[]{:S(2)}, u32[]{:S(2)}) async-start(bf16[4,32,12,128]{3,2,0,1:T(8,128)(2,1)} %copy.45), calls=%async_computation.3 | async-start | bytes 1048576 | tf_op jit(solution)/shard_map/all_to_all | solution.py:62
  76.3 71.7 %all-gather.2.cloned.1.call-done = bf16[1536,3072]{1,0:T(8,128)(2,1)} async-done(((bf16[96,3072]{1,0:T(8,128)(2,1)}), bf16[1536,3072]{1,0:T(8,128)(2,1)}) %all-gather.2.cloned.1.call-update) | async-done | bytes 9437200 | tf_op jit(solution)/shard_map/all_gather | solution.py:53
  148.0 0.0 copy-done
  148.0 6.9 %convolution_convert_fusion = bf16[128,1536]{1,0:T(8,128)(2,1)S(1)} fusion(bf16[128,3072]{1,0:T(8,128)(2,1)S(1)} %bitcast.71, bf16[1536,3072]{1,0:T(8,128)(2,1)} %all-gather.2.cloned.1.call-done), kind=kOutput, calls=%fused_computation.1 | convolution fusion | flops 1208156160 | bytes 10616832 | tf_op jit(solution)/shard_map/dot_general | solution.py:51
  154.9 0.3 reshape.88
  155.2 1.1 copy.43
  156.2 0.0 all-to-all-done.3
  156.2 7.6 %all-to-all-start.2 = ((bf16[4,32,12,128]{3,0,2,1:T(4,128)(2,1)}), bf16[4,32,12,128]{3,0,2,1:T(4,128)(2,1)S(1)}, u32[]{:S(2)}, u32[]{:S(2)}) async-start(bf16[4,32,12,128]{3,0,2,1:T(4,128)(2,1)} %copy.43), calls=%async_computation.2 | async-start | bytes 786432 | tf_op jit(solution)/shard_map/all_to_all | solution.py:63
  163.8 0.2 copy.40
  164.0 0.2 copy.42
  164.1 0.2 copy.46
  164.3 0.5 fusion.16
  164.8 0.0 copy-start.1
  164.8 12.3 %all-to-all-done.2 = bf16[4,32,12,128]{3,0,2,1:T(4,128)(2,1)S(1)} async-done(((bf16[4,32,12,128]{3,0,2,1:T(4,128)(2,1)}), bf16[4,32,12,128]{3,0,2,1:T(4,128)(2,1)S(1)}, u32[]{:S(2)}, u32[]{:S(2)}) %all-to-all-start.2) | async-done | bytes 393248 | tf_op jit(solution)/shard_map/all_to_all | solution.py:63
  177.1 0.2 copy.44
  177.3 0.5 fusion.7
  177.8 0.0 copy-done.1
  177.8 1.5 fusion.4
  179.3 0.3 fusion.10
  179.6 1.2 copy.51
  180.8 6.1 %all-to-all-start.4 = ((bf16[128,1,12,128]{3,2,1,0:T(8,128)(2,1)}), bf16[128,1,12,128]{3,2,1,0:T(8,128)(2,1)S(1)}, u32[]{:S(2)}, u32[]{:S(2)}) async-start(bf16[128,1,12,128]{3,2,1,0:T(8,128)(2,1)} %copy.51), calls=%async_computation.4 | async-start | bytes 1048576 | tf_op jit(solution)/shard_map/all_to_all | solution.py:41
  187.0 0.4 fusion.9
  187.4 1.2 copy.54
  188.6 13.4 %all-to-all-done.4 = bf16[128,1,12,128]{3,2,1,0:T(8,128)(2,1)S(1)} async-done(((bf16[128,1,12,128]{3,2,1,0:T(8,128)(2,1)}), bf16[128,1,12,128]{3,2,1,0:T(8,128)(2,1)S(1)}, u32[]{:S(2)}, u32[]{:S(2)}) %all-to-all-start.4) | async-done | bytes 393248 | tf_op jit(solution)/shard_map/all_to_all | solution.py:41
  202.0 7.3 %all-to-all-start.5 = ((bf16[128,1,12,128]{3,2,1,0:T(8,128)(2,1)}), bf16[128,1,12,128]{3,2,1,0:T(8,128)(2,1)S(1)}, u32[]{:S(2)}, u32[]{:S(2)}) async-start(bf16[128,1,12,128]{3,2,1,0:T(8,128)(2,1)} %copy.54), calls=%async_computation.5 | async-start | bytes 1048576 | tf_op jit(solution)/shard_map/all_to_all | solution.py:42
  209.3 1.6 fusion.8
  210.8 1.2 copy.58
  212.0 12.3 %all-to-all-done.5 = bf16[128,1,12,128]{3,2,1,0:T(8,128)(2,1)S(1)} async-done(((bf16[128,1,12,128]{3,2,1,0:T(8,128)(2,1)}), bf16[128,1,12,128]{3,2,1,0:T(8,128)(2,1)S(1)}, u32[]{:S(2)}, u32[]{:S(2)}) %all-to-all-start.5) | async-done | bytes 393248 | tf_op jit(solution)/shard_map/all_to_all | solution.py:42
  224.3 7.2 %all-to-all-start.6 = ((bf16[128,1,12,128]{3,2,1,0:T(8,128)(2,1)}), bf16[128,1,12,128]{3,2,1,0:T(8,128)(2,1)S(1)}, u32[]{:S(2)}, u32[]{:S(2)}) async-start(bf16[128,1,12,128]{3,2,1,0:T(8,128)(2,1)} %copy.58), calls=%async_computation.6 | async-start | bytes 1048576 | tf_op jit(solution)/shard_map/all_to_all | solution.py:43
  231.5 0.1 copy.52
  231.7 0.8 copy.60
  232.5 0.1 copy.55
  232.6 0.8 copy.61
  233.4 13.2 %all-to-all-done.6 = bf16[128,1,12,128]{3,2,1,0:T(8,128)(2,1)S(1)} async-done(((bf16[128,1,12,128]{3,2,1,0:T(8,128)(2,1)}), bf16[128,1,12,128]{3,2,1,0:T(8,128)(2,1)S(1)}, u32[]{:S(2)}, u32[]{:S(2)}) %all-to-all-start.6) | async-done | bytes 393248 | tf_op jit(solution)/shard_map/all_to_all | solution.py:43
  246.6 0.1 copy.59
  246.7 0.8 copy.62
Async XLA Ops:
  7.2 140.8 %copy-start = (bf16[4,32,3072]{2,1,0:T(8,128)(2,1)S(1)}, bf16[4,32,3072]{2,1,0:T(8,128)(2,1)}, u32[]{:S(2)}) copy-start(bf16[4,32,3072]{2,1,0:T(8,128)(2,1)} %param.8) | copy-start | bytes 2359300
  7.2 140.8 %all-gather.2.cloned.1.call-start = ((), (), s32[]{:S(2)}) async-start(), calls=%async_computation.7 | async-start | bytes 10027008 | tf_op jit(solution)/shard_map/all_gather | solution.py:53
  9.9 35.6 %all-to-all-start = ((bf16[4,32,12,128]{3,2,0,1:T(8,128)(2,1)}), bf16[4,32,12,128]{3,2,0,1:T(8,128)(2,1)S(1)}, u32[]{:S(2)}, u32[]{:S(2)}) async-start(bf16[4,32,12,128]{3,2,0,1:T(8,128)(2,1)} %copy.39), calls=%async_computation | async-start | bytes 1048576 | tf_op jit(solution)/shard_map/all_to_all | solution.py:60
  45.5 22.3 %all-to-all-start.1 = ((bf16[4,32,12,128]{3,2,0,1:T(8,128)(2,1)}), bf16[4,32,12,128]{3,2,0,1:T(8,128)(2,1)S(1)}, u32[]{:S(2)}, u32[]{:S(2)}) async-start(bf16[4,32,12,128]{3,2,0,1:T(8,128)(2,1)} %copy.41), calls=%async_computation.1 | async-start | bytes 1048576 | tf_op jit(solution)/shard_map/all_to_all | solution.py:61
  67.8 88.4 %all-to-all-start.3 = ((bf16[4,32,12,128]{3,2,0,1:T(8,128)(2,1)}), bf16[4,32,12,128]{3,2,0,1:T(8,128)(2,1)S(1)}, u32[]{:S(2)}, u32[]{:S(2)}) async-start(bf16[4,32,12,128]{3,2,0,1:T(8,128)(2,1)} %copy.45), calls=%async_computation.3 | async-start | bytes 1048576 | tf_op jit(solution)/shard_map/all_to_all | solution.py:62
  156.2 20.9 %all-to-all-start.2 = ((bf16[4,32,12,128]{3,0,2,1:T(4,128)(2,1)}), bf16[4,32,12,128]{3,0,2,1:T(4,128)(2,1)S(1)}, u32[]{:S(2)}, u32[]{:S(2)}) async-start(bf16[4,32,12,128]{3,0,2,1:T(4,128)(2,1)} %copy.43), calls=%async_computation.2 | async-start | bytes 786432 | tf_op jit(solution)/shard_map/all_to_all | solution.py:63
  164.8 13.0 %copy-start.1 = (f32[12,128,128]{1,2,0:T(8,128)}, f32[12,128,128]{1,2,0:T(8,128)S(1)}, u32[]{:S(2)}) copy-start(f32[12,128,128]{1,2,0:T(8,128)S(1)} %get-tuple-element.10) | copy-start | bytes 2359300
  180.8 21.2 %all-to-all-start.4 = ((bf16[128,1,12,128]{3,2,1,0:T(8,128)(2,1)}), bf16[128,1,12,128]{3,2,1,0:T(8,128)(2,1)S(1)}, u32[]{:S(2)}, u32[]{:S(2)}) async-start(bf16[128,1,12,128]{3,2,1,0:T(8,128)(2,1)} %copy.51), calls=%async_computation.4 | async-start | bytes 1048576 | tf_op jit(solution)/shard_map/all_to_all | solution.py:41
  202.0 22.3 %all-to-all-start.5 = ((bf16[128,1,12,128]{3,2,1,0:T(8,128)(2,1)}), bf16[128,1,12,128]{3,2,1,0:T(8,128)(2,1)S(1)}, u32[]{:S(2)}, u32[]{:S(2)}) async-start(bf16[128,1,12,128]{3,2,1,0:T(8,128)(2,1)} %copy.54), calls=%async_computation.5 | async-start | bytes 1048576 | tf_op jit(solution)/shard_map/all_to_all | solution.py:42
  224.3 22.3 %all-to-all-start.6 = ((bf16[128,1,12,128]{3,2,1,0:T(8,128)(2,1)}), bf16[128,1,12,128]{3,2,1,0:T(8,128)(2,1)S(1)}, u32[]{:S(2)}, u32[]{:S(2)}) async-start(bf16[128,1,12,128]{3,2,1,0:T(8,128)(2,1)} %copy.58), calls=%async_computation.6 | async-start | bytes 1048576 | tf_op jit(solution)/shard_map/all_to_all | solution.py:43
Sparse Core Ops, SparseCore 0:
  11.3 136.6 all-gather.1
where the time goes:
time: 257 us; the launch traced here: 254 us
  waiting for transfers between devices  155 us (60%)
  starting transfers between devices  59.6 us (23%)
  local copies, waits for them, and re-layouts  14.3 us (6%)
  between operations  14.2 us (6%)
  matrix products  11.7 us (5%)
    all_gather x1, waiting for transfers between devices, body(): lax.all_gather(out_proj, 'fsdp', axis=0, tiled=True)  71.7 us
    all_to_all x1, waiting for transfers between devices, body(): lax.all_to_all(queries, 'tm', split_axis=1, concat_axis=0, tiled=True)  19.3 us
    all_to_all x1, starting transfers between devices, body(): lax.all_to_all(queries, 'tm', split_axis=1, concat_axis=0, tiled=True)  14.3 us
    all_to_all x1, waiting for transfers between devices, send_back(): lax.all_to_all(grads[0], 'tm', split_axis=0, concat_axis=1, tiled=True)  13.4 us
    all_to_all x1, waiting for transfers between devices, send_back(): lax.all_to_all(grads[2], 'tm', split_axis=0, concat_axis=1, tiled=True)  13.2 us
    all_to_all x1, waiting for transfers between devices, body(): lax.all_to_all(grad_attn, 'tm', split_axis=1, concat_axis=0, tiled=True)  12.3 us
    all_to_all x1, waiting for transfers between devices, send_back(): lax.all_to_all(grads[1], 'tm', split_axis=0, concat_axis=1, tiled=True)  12.3 us
    all_to_all x1, waiting for transfers between devices, body(): lax.all_to_all(key_states, 'tm', split_axis=1, concat_axis=0, tiled=True)  11.8 us
  transfers between devices with their start and end apart: 8, of which 7 were waited for; matrix products, arithmetic and copies ran while one was open for 8% of the time, Pallas kernels for 0%

commit v1 on v0

v1 whole, which is shorter than its diff:
```python
import jax
import jax.numpy as jnp
from jax import lax
from jax.experimental import pallas as pl
from jax.experimental.pallas import tpu as pltpu
from jax.sharding import PartitionSpec as P

MESH = pl.DeviceIdType.MESH
F32 = jnp.float32
BF16 = jnp.bfloat16

NX, NYH, NC = 4, 2, 2
NYL, NZ = 4, 8
NT = NYL * NZ

OWN_O, OWN_E, L_O, L_E, R_O, R_E, D_O, D_E = range(8)


def mm(a, b, ca, cb):
    return lax.dot_general(a, b, (((ca,), (cb,)), ((), ())), preferred_element_type=F32)


def kernel(q_ref, k_ref, v_ref, x_ref, w_ref, dq_ref, dk_ref, dv_ref,
           wbuf, xp, snd, rcv, gs, gr, os, orr,
           own_sem, w_recv, w_recv2, sib_recv, sib_send, w_send,
           qkv_s, qkv_r, g_s, g_r, o_s, o_r):
    t = lax.axis_index("tm")
    f = lax.axis_index("fsdp")
    yl, z = t // NZ, t % NZ
    x, yh, c = f // (NYH * NC), (f // NC) % NYH, f % NC
    heads = q_ref.shape[1]
    frames, pos = x_ref.shape[0], x_ref.shape[1]
    rows = frames * pos
    group = heads // NX
    wrows = w_ref.shape[0]
    half = wrows // 2
    scale = q_ref.shape[-1] ** (-0.5)

    def fs(xx, yy, cc):
        return xx * (NYH * NC) + yy * NC + cc

    right, left, far = (x + 1) % NX, (x + NX - 1) % NX, (x + 2) % NX
    sib = (t, fs(x, yh, 1 - c))
    to_right = (t, fs(right, yh, c))
    to_left = (t, fs(left, yh, c))
    mirror = ((NYL - 1 - yl) * NZ + z, fs(x, 1 - yh, c))
    edge = jnp.logical_or(yl == 0, yl == NYL - 1)
    inner = (jnp.where(yl == 0, 1, NYL - 2) * NZ + z, f)

    def peer(d):
        return ((yl + d % NYL) % NYL) * NZ + (z + 5 * (d // NYL)) % NZ

    barrier = pltpu.get_barrier_semaphore()

    @pl.loop(1, NT)
    def _(d):
        pl.semaphore_signal(barrier, inc=1, device_id=(peer(d), f), device_id_type=MESH)

    for other in (sib, to_right, to_left, mirror):
        pl.semaphore_signal(barrier, inc=1, device_id=other, device_id_type=MESH)
    pl.semaphore_wait(barrier, NT - 1 + 4)

    def block(xx, yy, first=0, count=wrows):
        start = pl.multiple_of((yy * NC + c) * wrows + first, 16)
        return wbuf.at[xx, pl.ds(start, count), :]

    def sib_block(xx, yy):
        start = pl.multiple_of((yy * NC + 1 - c) * wrows, 16)
        return wbuf.at[xx, pl.ds(start, wrows), :]

    def rcopy(src, dst, ssem, rsem, dev):
        return pltpu.make_async_remote_copy(
            src_ref=src, dst_ref=dst, send_sem=ssem, recv_sem=rsem,
            device_id=dev, device_id_type=MESH)

    def arrived(ref, sem):
        pltpu.make_async_copy(ref, ref, sem).wait()

    sent = []

    def send(src, dst, ssem, rsem, dev):
        cp = rcopy(src, dst, ssem, rsem, dev)
        cp.start()
        sent.append(cp)

    own_o = block(x, yh)
    own_copy = pltpu.make_async_copy(w_ref, own_o, own_sem)
    own_copy.start()
    send(w_ref, own_o, w_send.at[0], w_recv.at[L_O], to_right)
    send(w_ref, own_o, w_send.at[1], w_recv.at[R_O], to_left)
    send(w_ref, own_o, sib_send.at[OWN_O], sib_recv.at[OWN_O], sib)
    to_mirror = [
        rcopy(w_ref.at[pl.ds(i * half, half), :], block(x, yh, i * half, half),
              w_send.at[2 + i], w_recv2.at[i], mirror)
        for i in range(2)
    ]

    @pl.when(edge)
    def _():
        for cp in to_mirror:
            cp.start()

    ri = lax.broadcasted_iota(jnp.int32, (rows, rows), 0)
    ci = lax.broadcasted_iota(jnp.int32, (rows, rows), 1)
    to_pos = ((ri % frames) * pos + ri // frames == ci).astype(F32).astype(BF16)
    to_frame = ((ri % pos) * frames + ri // pos == ci).astype(F32).astype(BF16)

    snd_v = snd.reshape(3, heads, rows, 128)
    rcv_v = rcv.reshape(3, heads, 128, 128)
    gs_v = gs.reshape(heads, rows, 128)
    gr_v = gr.reshape(heads, 128, 128)
    os_v = os.reshape(3, heads, 128, 128)
    orr_v = orr.reshape(3, heads, rows, 128)

    @pl.loop(0, heads)
    def _(h):
        for i, ref in enumerate((q_ref, k_ref, v_ref)):
            snd_v[i, h] = mm(to_pos, ref[:, h].reshape(rows, 128), 1, 0).astype(BF16)

    pltpu.make_async_copy(snd.at[:, :, t], rcv.at[:, :, t], qkv_r).start()

    @pl.loop(1, NT)
    def _(d):
        p = peer(d)
        rcopy(snd.at[:, :, p], rcv.at[:, :, t], qkv_s, qkv_r, (p, f)).start()

    @pl.loop(0, x_ref.shape[2] // 512)
    def _(i):
        cols = pl.ds(pl.multiple_of(i * 512, 512), 512)
        xp[:, cols] = mm(to_pos, x_ref[:, :, cols].reshape(rows, 512), 1, 0).astype(BF16)

    def share(which, xx, yy):
        send(block(xx, yy), block(xx, yy), sib_send.at[which], sib_recv.at[which], sib)

    arrived(block(left, yh), w_recv.at[L_O])
    send(block(left, yh, 0, half), block(left, yh, 0, half), w_send.at[4], w_recv.at[D_O], to_right)
    share(L_O, left, yh)
    arrived(block(right, yh), w_recv.at[R_O])
    send(block(right, yh, half, half), block(right, yh, half, half), w_send.at[5], w_recv2.at[2], to_left)
    share(R_O, right, yh)

    oh = 1 - yh
    to_inner = [
        rcopy(block(x, oh, i * half, half), block(x, oh, i * half, half),
              w_send.at[6 + i], w_recv2.at[i], inner)
        for i in range(2)
    ]
    for i in range(2):
        arrived(block(x, oh, i * half, half), w_recv2.at[i])

        @pl.when(edge)
        def _():
            to_inner[i].start()

    send(block(x, oh), block(x, oh), w_send.at[8], w_recv.at[L_E], to_right)
    send(block(x, oh), block(x, oh), w_send.at[9], w_recv.at[R_E], to_left)
    share(OWN_E, x, oh)

    def project(xx):
        acc = mm(xp[...], wbuf[xx], 1, 1)
        for i in range(group):
            gs_v[xx * group + i] = acc[:, i * 128:(i + 1) * 128].astype(BF16)

    def send_g(step, xx):
        hs = pl.ds(xx * group, group)
        pltpu.make_async_copy(gs.at[hs, t], gr.at[hs, t], g_r.at[step]).start()

        @pl.loop(1, NT)
        def _(d):
            p = peer(d)
            rcopy(gs.at[hs, p], gr.at[hs, t], g_s.at[step], g_r.at[step], (p, f)).start()

    def attend(step, xx):
        hs = pl.ds(xx * group, group)
        arrived(gr.at[hs], g_r.at[step])
        for i in range(group):
            h = xx * group + i
            q, k, v, g = rcv_v[0, h], rcv_v[1, h], rcv_v[2, h], gr_v[h]
            s = mm(k, q, 1, 1) * scale
            e = jnp.exp(s - jnp.max(s, axis=0, keepdims=True))
            probs = e * (1.0 / jnp.sum(e, axis=0, keepdims=True))
            pb = probs.astype(BF16)
            dp = mm(v, g, 1, 1)
            delta = jnp.sum(pb.astype(F32) * dp, axis=0, keepdims=True)
            ds = (probs * (dp - delta)).astype(BF16)
            os_v[0, h] = (mm(ds, k, 0, 0) * scale).astype(BF16)
            os_v[1, h] = (mm(ds, q, 1, 0) * scale).astype(BF16)
            os_v[2, h] = mm(pb, g, 1, 0).astype(BF16)
        pltpu.make_async_copy(os.at[:, hs, t], orr.at[:, hs, t], o_r.at[step]).start()

        @pl.loop(1, NT)
        def _(d):
            p = peer(d)
            rcopy(os.at[:, hs, p], orr.at[:, hs, t], o_s.at[step], o_r.at[step], (p, f)).start()

    def finish(step, xx):
        hs = pl.ds(xx * group, group)
        arrived(orr.at[:, hs], o_r.at[step])
        for j, ref in enumerate((dq_ref, dk_ref, dv_ref)):
            for i in range(group):
                h = xx * group + i
                ref[:, h] = mm(to_frame, orr_v[j, h], 1, 0).astype(BF16).reshape(frames, pos, 128)

    own_copy.wait()
    arrived(sib_block(x, yh), sib_recv.at[OWN_O])
    arrived(sib_block(x, oh), sib_recv.at[OWN_E])
    project(x)
    send_g(0, x)

    arrived(block(left, oh), w_recv.at[L_E])
    send(block(left, oh, 0, half), block(left, oh, 0, half), w_send.at[10], w_recv.at[D_E], to_right)
    share(L_E, left, oh)
    arrived(block(right, oh), w_recv.at[R_E])
    send(block(right, oh, half, half), block(right, oh, half, half), w_send.at[11], w_recv2.at[3], to_left)
    share(R_E, right, oh)
    arrived(block(far, yh, 0, half), w_recv.at[D_O])
    arrived(block(far, yh, half, half), w_recv2.at[2])
    share(D_O, far, yh)

    arrived(sib_block(right, yh), sib_recv.at[R_O])
    arrived(sib_block(right, oh), sib_recv.at[R_E])
    project(right)
    send_g(1, right)
    arrived(sib_block(left, yh), sib_recv.at[L_O])
    arrived(sib_block(left, oh), sib_recv.at[L_E])
    project(left)
    send_g(2, left)

    arrived(rcv, qkv_r)
    attend(0, x)
    arrived(block(far, oh, 0, half), w_recv.at[D_E])
    arrived(block(far, oh, half, half), w_recv2.at[3])
    share(D_E, far, oh)
    attend(1, right)
    arrived(sib_block(far, yh), sib_recv.at[D_O])
    arrived(sib_block(far, oh), sib_recv.at[D_E])
    project(far)
    send_g(3, far)
    attend(2, left)
    attend(3, far)

    for step, xx in enumerate((x, right, left, far)):
        finish(step, xx)

    for cp in sent:
        cp.wait_send()

    @pl.when(edge)
    def _():
        for cp in to_mirror + to_inner:
            cp.wait_send()

    rest = snd.at[:, :, pl.ds(0, NT - 1)]
    pltpu.make_async_copy(rest, rest, qkv_s).wait()
    for step, xx in enumerate((x, right, left, far)):
        hs = pl.ds(xx * group, group)
        rest = gs.at[hs, pl.ds(0, NT - 1)]
        pltpu.make_async_copy(rest, rest, g_s.at[step]).wait()
        rest = os.at[:, hs, pl.ds(0, NT - 1)]
        pltpu.make_async_copy(rest, rest, o_s.at[step]).wait()


def body(queries, key_states, value_states, out_grad, out_proj):
    frames, pos, heads, size = queries.shape
    wrows, width = out_proj.shape
    vmem = pl.BlockSpec(memory_space=pltpu.VMEM)
    dma = pltpu.SemaphoreType.DMA

    def turn(a):
        return jnp.transpose(a, (0, 2, 1, 3))

    outs = pl.pallas_call(
        kernel,
        out_shape=[jax.ShapeDtypeStruct((frames, heads, pos, size), BF16)] * 3,
        in_specs=[vmem] * 5,
        out_specs=[vmem] * 3,
        scratch_shapes=[
            pltpu.VMEM((NX, NYH * NC * wrows, width), BF16),
            pltpu.VMEM((frames * pos, width), BF16),
            pltpu.VMEM((3, heads, pos, frames, size), BF16),
            pltpu.VMEM((3, heads, NT, frames, size), BF16),
            pltpu.VMEM((heads, pos, frames, size), BF16),
            pltpu.VMEM((heads, NT, frames, size), BF16),
            pltpu.VMEM((3, heads, NT, frames, size), BF16),
            pltpu.VMEM((3, heads, pos, frames, size), BF16),
            dma, dma((8,)), dma((4,)), dma((8,)), dma((8,)), dma((12,)),
            dma, dma, dma((4,)), dma((4,)), dma((4,)), dma((4,)),
        ],
        compiler_params=pltpu.CompilerParams(
            collective_id=0, has_side_effects=True, vmem_limit_bytes=48 << 20),
    )(turn(queries), turn(key_states), turn(value_states), out_grad, out_proj)
    return tuple(turn(o) for o in outs)


def solution(mesh):
    return jax.shard_map(
        body,
        mesh=mesh,
        in_specs=(
            P("tm", "fsdp", None, None),
            P("tm", "fsdp", None, None),
            P("tm", "fsdp", None, None),
            P("tm", "fsdp", None),
            P("fsdp", None),
        ),
        out_specs=(
            P("tm", "fsdp", None, None),
            P("tm", "fsdp", None, None),
            P("tm", "fsdp", None, None),
        ),
        check_vma=False,
    )
```

time: 257 us -> 112 us (0.44)
  waiting for transfers between devices: 155 us -> 0 us
  Pallas kernels: 0 us -> 103 us
  starting transfers between devices: 59.6 us -> 0 us
  between operations: 14.2 us -> 0.65 us
  matrix products: 11.7 us -> 0 us
  local copies, waits for them, and re-layouts: 14.3 us -> 7.41 us
    pallas_call x0 -> x1, Pallas kernels: none -> 103 us  [body(): pl.pallas_call(kernel, out_shape=[jax.ShapeDtypeStruct((frames, heads, po...]
    all_to_all x7 -> x0, waiting for transfers between devices: 82.2 us -> none  [the longest x1 19.3 us: body(): lax.all_to_all(queries, 'tm', split_axis=1, concat_axis=0, tiled=True)]
    all_gather x1 -> x0, waiting for transfers between devices: 71.7 us -> none  [body(): lax.all_gather(out_proj, 'fsdp', axis=0, tiled=True)]
    all_to_all x7 -> x0, starting transfers between devices: 59.5 us -> none  [the longest x1 14.3 us: body(): lax.all_to_all(queries, 'tm', split_axis=1, concat_axis=0, tiled=True)]
    dot_general x6 -> x0, matrix products: 11.2 us -> none  [the longest x1 6.9 us: body(): lax.dot_general(flat, lax.all_gather(out_proj, 'fsdp', axis=0, tiled=True...]
    convert_element_type x3 -> x0, local copies, waits for them, and re-layouts: 3.6 us -> none  [the longest x1 1.21 us: attend_back(): key_grad = (jnp.einsum('phfg,fphd->gphd', dscores, query_block, preferred...]
    unnamed x10 -> x13, local copies, waits for them, and re-layouts: 8.38 us -> 7.41 us
  transfers between devices with their start and end apart: 8 -> 0, of which waited for: 7 -> 0; matrix products, arithmetic and copies ran while one was open for 8% -> 0% of each run, Pallas kernels for 0% -> 0%
where the time goes in v1:
time: 112 us; the launch traced here: 111 us
  Pallas kernels  103 us (92%)
  local copies, waits for them, and re-layouts  7.41 us (7%)
    pallas_call x1, Pallas kernels, body(): pl.pallas_call(kernel, out_shape=[jax.ShapeDtypeStruct((frames, heads, po...  103 us
    unnamed x13, local copies, waits for them, and re-layouts  7.41 us

profile of v1, /device:TPU:1, one launch (start us, length us, event | category | flops | bytes accessed | tf_op | source)
XLA Modules:
  0.0 111.3 jit_solution(10862292923554290805)
XLA Ops:
  0.6 0.0 copy-start
  0.6 1.1 %copy-done = bf16[4,32,3072]{2,1,0:T(8,128)(2,1)S(1)} copy-done((bf16[4,32,3072]{2,1,0:T(8,128)(2,1)S(1)}, bf16[4,32,3072]{2,1,0:T(8,128)(2,1)}, u32[]{:S(2)}) %copy-start) | copy-done | bytes 786456
  1.8 0.0 copy-start.1
  1.8 1.1 copy-done.1
  2.8 0.0 copy-start.2
  2.8 1.0 copy-done.2
  3.8 0.0 copy-start.3
  3.8 1.0 copy-done.3
  4.8 0.0 copy-start.4
  4.8 1.0 copy-done.4
  5.8 103.3 %shard_map.76 = (bf16[4,12,32,128]{3,2,1,0:T(8,128)(2,1)S(1)}, bf16[4,12,32,128]{3,2,1,0:T(8,128)(2,1)S(1)}, bf16[4,12,32,128]{3,2,1,0:T(8,128)(2,1)S(1)}) custom-call(bf16[4,12,32,128]{3,2,1,0:T(8,128)(2,1)S(1)} %bitcast.6, bf16[4,12,32,128]{3,2,1,0:T(8,128)(2,1)S(1)} %bitcast.7, bf16[4,12,32,128]{3,2,1,0:T(8,128)(2,1)S(1)} %bitcast.8, ...), custom_call_target="tpu_custom_call" | custom-call | tf_op jit(solution)/shard_map/pallas_call | solution.py:272
  109.1 0.7 copy.11
  109.8 0.7 copy.12
  110.6 0.7 copy.13
Async XLA Ops:
  0.6 1.1 %copy-start = (bf16[4,32,3072]{2,1,0:T(8,128)(2,1)S(1)}, bf16[4,32,3072]{2,1,0:T(8,128)(2,1)}, u32[]{:S(2)}) copy-start(bf16[4,32,3072]{2,1,0:T(8,128)(2,1)} %x_ref.1) | copy-start | bytes 2359300
  1.8 1.1 copy-start.1
  2.8 1.0 copy-start.2
  3.8 1.0 copy-start.3
  4.8 1.0 copy-start.4

commit v2 on v0

v2 whole, which is shorter than its diff:
```python
import jax
import jax.numpy as jnp
from jax import lax
from jax.experimental import pallas as pl
from jax.experimental.pallas import tpu as pltpu
from jax.sharding import PartitionSpec as P

MESH = pl.DeviceIdType.MESH
F32 = jnp.float32
BF16 = jnp.bfloat16

NX, NYH, NC = 4, 2, 2
NYL, NZ = 4, 8
NT = NYL * NZ

NE = 6


def mm(a, b, ca, cb):
    return lax.dot_general(a, b, (((ca,), (cb,)), ((), ())), preferred_element_type=F32)


def kernel(q_ref, k_ref, v_ref, x_ref, w_ref, dq_ref, dk_ref, dv_ref,
           qin, wbuf, xbuf, snd, rcv, gst_a, gs_a, gr_a, os_a, or_a, gst_b, gs_b, gr_b, os_b, or_b, out,
           in_sem, w_send, sib_send, sib_recv, e_recv, x_send, x_recv, xh_recv,
           gx_send, gx_recv, out_sem, qkv_s, qkv_r, g_s, g_r, o_s, o_r):
    t = lax.axis_index("tm")
    f = lax.axis_index("fsdp")
    yl, z = t // NZ, t % NZ
    x, yh, c = f // (NYH * NC), (f // NC) % NYH, f % NC
    frames, heads, pos, size = q_ref.shape
    rows = frames * pos
    group = heads // NX
    wrows = w_ref.shape[0]
    part = wrows // NE
    scale = size ** (-0.5)

    def fs(xx, yy, cc):
        return xx * (NYH * NC) + yy * NC + cc

    right, left, far = (x + 1) % NX, (x + NX - 1) % NX, (x + 2) % NX
    oh = 1 - yh
    sib = (t, fs(x, yh, 1 - c))

    def along_x(xx):
        return (t, fs(xx, yh, c))

    mirror = ((NYL - 1 - yl) * NZ + z, fs(x, oh, c))
    edge = jnp.logical_or(yl == 0, yl == NYL - 1)
    inner = (jnp.where(yl == 0, 1, NYL - 2) * NZ + z, f)

    def peer(d):
        return ((yl + d // NZ) % NYL) * NZ + (z + 5 * (d % NZ)) % NZ

    def block(yy, cc, i=0, n=NE):
        start = pl.multiple_of((yy * NC + cc) * wrows + i * part, 8)
        return wbuf.at[pl.ds(start, n * part), :]

    loads = [pltpu.make_async_copy(src, qin.at[i], in_sem.at[i])
             for i, src in enumerate((q_ref, k_ref, v_ref))]
    loads.append(pltpu.make_async_copy(w_ref, block(yh, c), in_sem.at[3]))
    loads.append(pltpu.make_async_copy(x_ref, xbuf.at[x], in_sem.at[4]))
    for cp in loads:
        cp.start()

    barrier = pltpu.get_barrier_semaphore()

    @pl.loop(1, NT)
    def _(d):
        pl.semaphore_signal(barrier, inc=1, device_id=(peer(d), f), device_id_type=MESH)

    others = (sib, along_x(right), along_x(left), along_x(far), mirror)
    for other in others:
        pl.semaphore_signal(barrier, inc=1, device_id=other, device_id_type=MESH)
    ri = lax.broadcasted_iota(jnp.int32, (rows, rows), 0)
    ci = lax.broadcasted_iota(jnp.int32, (rows, rows), 1)
    to_pos = ((ri % frames) * pos + ri // frames == ci).astype(F32).astype(BF16)
    to_frame = ((ri % pos) * frames + ri // pos == ci).astype(F32).astype(BF16)

    snd_v = snd.reshape(3, heads, rows, size)
    rcv_v = rcv.reshape(3, heads, NT * frames, size)

    for cp in loads[:3]:
        cp.wait()

    @pl.loop(0, heads)
    def _(h):
        for i in range(3):
            snd_v[i, h] = mm(to_pos, qin[i, :, h].reshape(rows, size), 1, 0).astype(BF16)

    pl.semaphore_wait(barrier, NT - 1 + len(others))

    def rcopy(src, dst, ssem, rsem, dev):
        return pltpu.make_async_remote_copy(
            src_ref=src, dst_ref=dst, send_sem=ssem, recv_sem=rsem,
            device_id=dev, device_id_type=MESH)

    def arrived(ref, sem):
        pltpu.make_async_copy(ref, ref, sem).wait()

    sent = []

    def send(src, dst, ssem, rsem, dev):
        cp = rcopy(src, dst, ssem, rsem, dev)
        cp.start()
        sent.append(cp)

    to_mirror = [
        rcopy(w_ref.at[pl.ds(i * part, part), :], block(yh, c, i, 1), w_send.at[i], e_recv.at[i], mirror)
        for i in range(NE)
    ]
    to_inner = [
        rcopy(block(oh, c, i, 1), block(oh, c, i, 1), w_send.at[NE + i], e_recv.at[i], inner)
        for i in range(NE)
    ]
    to_sib = [
        rcopy(block(oh, c, i, 1), block(oh, c, i, 1), sib_send.at[i], sib_recv.at[i], sib)
        for i in range(NE)
    ]

    @pl.when(edge)
    def _():
        for cp in to_mirror:
            cp.start()

    send(x_ref, xbuf.at[x], x_send.at[0], x_recv.at[0], along_x(right))
    send(x_ref, xbuf.at[x], x_send.at[1], x_recv.at[1], along_x(left))
    send(w_ref, block(yh, c), sib_send.at[NE], sib_recv.at[NE], sib)

    pltpu.make_async_copy(snd.at[:, :, t], rcv.at[:, :, t], qkv_r).start()

    @pl.loop(1, NT)
    def _(d):
        p = peer(d)
        rcopy(snd.at[:, :, p], rcv.at[:, :, t], qkv_s, qkv_r, (p, f)).start()

    order = (x, right, left, far)
    first = (group - 1) * yh
    rest = 1 - yh
    nb = group - 1

    class Phase:
        def __init__(self, gst, gs, gr, os, orr, count, head, sems):
            n = NX * count
            self.gst, self.gs, self.gr, self.os, self.orr = gst, gs, gr, os, orr
            self.gst_v = gst.reshape(NX * count, rows, size)
            self.gs_v = gs.reshape(n, rows, size)
            self.gr_v = gr.reshape(n, NT * frames, size)
            self.os_v = os.reshape(3, n, NT * frames, size)
            self.orr_v = orr.reshape(3, n, rows, size)
            self.count, self.head, self.sems = count, head, sems

    pa = Phase(gst_a, gs_a, gr_a, os_a, or_a, 1, first, 0)
    pb = Phase(gst_b, gs_b, gr_b, os_b, or_b, nb, rest, 3)

    def project(ph, xx):
        ws = pl.ds(pl.multiple_of(ph.head * size, size), ph.count * size)
        acc = mm(xbuf[xx].reshape(rows, -1), wbuf[ws, :], 1, 1).astype(BF16)
        return mm(to_pos, acc, 1, 0).astype(BF16)

    def own_g(ph):
        acc = project(ph, x)
        for j in range(ph.count):
            ph.gs_v[j] = acc[:, j * size:(j + 1) * size]

    back = (2, 1, 3)

    def return_g(ph, i):
        xx = order[i + 1]
        acc = project(ph, xx)
        for j in range(ph.count):
            ph.gst_v[i * ph.count + j] = acc[:, j * size:(j + 1) * size]
        send(ph.gst.at[pl.ds(i * ph.count, ph.count)], ph.gs.at[pl.ds(back[i] * ph.count, ph.count)],
             gx_send.at[ph.sems + i], gx_recv.at[ph.sems + back[i] - 1], along_x(xx))

    def take_g(ph, slot):
        arrived(ph.gs.at[pl.ds(slot * ph.count, ph.count)], gx_recv.at[ph.sems + slot - 1])

    steps = []

    def send_g(ph, lo, n):
        step = len(steps)
        hs = pl.ds(lo * ph.count, n * ph.count)
        steps.append((ph, lo, n, hs))
        pltpu.make_async_copy(ph.gs.at[hs, t], ph.gr.at[hs, t], g_r.at[step]).start()

        @pl.loop(1, NT)
        def _(d):
            p = peer(d)
            rcopy(ph.gs.at[hs, p], ph.gr.at[hs, t], g_s.at[step], g_r.at[step], (p, f)).start()

    def attend(step):
        ph, lo, n, hs = steps[step]
        arrived(ph.gr.at[hs], g_r.at[step])
        for i in range(lo, lo + n):
            for j in range(ph.count):
                h, m = order[i] * group + ph.head + j, i * ph.count + j
                q, k, v, g = rcv_v[0, h], rcv_v[1, h], rcv_v[2, h], ph.gr_v[m]
                s = mm(k, q, 1, 1) * scale
                e = jnp.exp(s - jnp.max(s, axis=0, keepdims=True))
                probs = e * (1.0 / jnp.sum(e, axis=0, keepdims=True))
                pb16 = probs.astype(BF16)
                dp = mm(v, g, 1, 1)
                delta = jnp.sum(pb16.astype(F32) * dp, axis=0, keepdims=True)
                ds = (probs * (dp - delta)).astype(BF16)
                ph.os_v[0, m] = (mm(ds, k, 0, 0) * scale).astype(BF16)
                ph.os_v[1, m] = (mm(ds, q, 1, 0) * scale).astype(BF16)
                ph.os_v[2, m] = mm(pb16, g, 1, 0).astype(BF16)
        pltpu.make_async_copy(ph.os.at[:, hs, t], ph.orr.at[:, hs, t], o_r.at[step]).start()

        @pl.loop(1, NT)
        def _(d):
            p = peer(d)
            rcopy(ph.os.at[:, hs, p], ph.orr.at[:, hs, t], o_s.at[step], o_r.at[step], (p, f)).start()

    stores = []

    def finish(step):
        ph, lo, n, hs = steps[step]
        arrived(ph.orr.at[:, hs], o_r.at[step])
        for j, ref in enumerate((dq_ref, dk_ref, dv_ref)):
            for i in range(lo, lo + n):
                start = order[i] * group + ph.head
                for u in range(ph.count):
                    out[j, :, start + u] = mm(to_frame, ph.orr_v[j, i * ph.count + u], 1, 0).astype(BF16).reshape(
                        frames, pos, size)
                cp = pltpu.make_async_copy(out.at[j, :, pl.ds(start, ph.count)], ref.at[:, pl.ds(start, ph.count)],
                                           out_sem.at[len(stores)])
                cp.start()
                stores.append(cp)

    loads[3].wait()
    loads[4].wait()
    arrived(block(yh, 1 - c), sib_recv.at[NE])
    own_g(pa)

    @pl.when(edge)
    def _():
        for i in range(NE):
            arrived(block(oh, c, i, 1), e_recv.at[i])
            to_inner[i].start()
            to_sib[i].start()

    hf = frames // 2
    arrived(xbuf.at[left], x_recv.at[0])
    low = xbuf.at[left, pl.ds(0, hf)]
    send(low, low, x_send.at[2], xh_recv.at[0], along_x(right))
    arrived(xbuf.at[right], x_recv.at[1])
    high = xbuf.at[right, pl.ds(hf, hf)]
    send(high, high, x_send.at[3], xh_recv.at[1], along_x(left))
    return_g(pa, 0)
    return_g(pa, 1)
    arrived(xbuf.at[far, pl.ds(0, hf)], xh_recv.at[0])
    arrived(xbuf.at[far, pl.ds(hf, hf)], xh_recv.at[1])
    return_g(pa, 2)

    @pl.when(jnp.logical_not(edge))
    def _():
        for i in range(NE):
            arrived(block(oh, c, i, 1), e_recv.at[i])
            to_sib[i].start()

    for slot in (1, 2, 3):
        take_g(pa, slot)
    send_g(pa, 0, 4)

    for i in range(NE):
        arrived(block(oh, 1 - c, i, 1), sib_recv.at[i])
    for i in range(3):
        return_g(pb, i)
    own_g(pb)
    take_g(pb, 1)
    send_g(pb, 0, 2)
    take_g(pb, 2)
    take_g(pb, 3)
    send_g(pb, 2, 2)

    arrived(rcv, qkv_r)
    for step in range(3):
        attend(step)
    for step in range(3):
        finish(step)
    for cp in stores:
        cp.wait()

    for cp in sent + to_sib:
        cp.wait_send()

    @pl.when(edge)
    def _():
        for cp in to_mirror + to_inner:
            cp.wait_send()

    others = snd.at[:, :, pl.ds(0, NT - 1)]
    pltpu.make_async_copy(others, others, qkv_s).wait()
    for step, (ph, lo, n, hs) in enumerate(steps):
        others = ph.gs.at[hs, pl.ds(0, NT - 1)]
        pltpu.make_async_copy(others, others, g_s.at[step]).wait()
        others = ph.os.at[:, hs, pl.ds(0, NT - 1)]
        pltpu.make_async_copy(others, others, o_s.at[step]).wait()


def body(queries, key_states, value_states, out_grad, out_proj):
    frames, pos, heads, size = queries.shape
    wrows, width = out_proj.shape
    hbm = pl.BlockSpec(memory_space=pltpu.HBM)
    dma = pltpu.SemaphoreType.DMA

    def turn(a):
        return jnp.transpose(a, (0, 2, 1, 3))

    def phase(count):
        n = NX * count
        return [pltpu.VMEM(shape, BF16) for shape in (
            (n, pos, frames, size), (n, pos, frames, size), (n, NT, frames, size),
            (3, n, NT, frames, size), (3, n, pos, frames, size))]

    outs = pl.pallas_call(
        kernel,
        out_shape=[jax.ShapeDtypeStruct((frames, heads, pos, size), BF16)] * 3,
        in_specs=[hbm] * 5,
        out_specs=[hbm] * 3,
        scratch_shapes=[
            pltpu.VMEM((3, frames, heads, pos, size), BF16),
            pltpu.VMEM((NYH * NC * wrows, width), BF16),
            pltpu.VMEM((NX, frames, pos, width), BF16),
            pltpu.VMEM((3, heads, pos, frames, size), BF16),
            pltpu.VMEM((3, heads, NT, frames, size), BF16),
            *phase(1),
            *phase(heads // NX - 1),
            pltpu.VMEM((3, frames, heads, pos, size), BF16),
            dma((5,)), dma((2 * NE,)), dma((NE + 1,)), dma((NE + 1,)), dma((NE,)),
            dma((4,)), dma((2,)), dma((2,)), dma((6,)), dma((6,)), dma((3 * heads,)),
            dma, dma, dma((3,)), dma((3,)), dma((3,)), dma((3,)),
        ],
        compiler_params=pltpu.CompilerParams(
            collective_id=0, has_side_effects=True, vmem_limit_bytes=60 << 20),
    )(turn(queries), turn(key_states), turn(value_states), out_grad, out_proj)
    return tuple(turn(o) for o in outs)


def solution(mesh):
    return jax.shard_map(
        body,
        mesh=mesh,
        in_specs=(
            P("tm", "fsdp", None, None),
            P("tm", "fsdp", None, None),
            P("tm", "fsdp", None, None),
            P("tm", "fsdp", None),
            P("fsdp", None),
        ),
        out_specs=(
            P("tm", "fsdp", None, None),
            P("tm", "fsdp", None, None),
            P("tm", "fsdp", None, None),
        ),
        check_vma=False,
    )
```

time: 257 us -> 95 us (0.37)
  waiting for transfers between devices: 155 us -> 0 us
  Pallas kernels: 0 us -> 89.5 us
  starting transfers between devices: 59.6 us -> 0 us
  between operations: 14.2 us -> 0.65 us
  matrix products: 11.7 us -> 0 us
  local copies, waits for them, and re-layouts: 14.3 us -> 3.7 us
    pallas_call x0 -> x1, Pallas kernels: none -> 89.5 us  [body(): pl.pallas_call(kernel, out_shape=[jax.ShapeDtypeStruct((frames, heads, po...]
    all_to_all x7 -> x0, waiting for transfers between devices: 82.2 us -> none  [the longest x1 19.3 us: body(): lax.all_to_all(queries, 'tm', split_axis=1, concat_axis=0, tiled=True)]
    all_gather x1 -> x0, waiting for transfers between devices: 71.7 us -> none  [body(): lax.all_gather(out_proj, 'fsdp', axis=0, tiled=True)]
    all_to_all x7 -> x0, starting transfers between devices: 59.5 us -> none  [the longest x1 14.3 us: body(): lax.all_to_all(queries, 'tm', split_axis=1, concat_axis=0, tiled=True)]
    dot_general x6 -> x0, matrix products: 11.2 us -> none  [the longest x1 6.9 us: body(): lax.dot_general(flat, lax.all_gather(out_proj, 'fsdp', axis=0, tiled=True...]
    unnamed x10 -> x7, local copies, waits for them, and re-layouts: 8.38 us -> 3.7 us
    convert_element_type x3 -> x0, local copies, waits for them, and re-layouts: 3.6 us -> none  [the longest x1 1.21 us: attend_back(): key_grad = (jnp.einsum('phfg,fphd->gphd', dscores, query_block, preferred...]
  transfers between devices with their start and end apart: 8 -> 0, of which waited for: 7 -> 0; matrix products, arithmetic and copies ran while one was open for 8% -> 0% of each run, Pallas kernels for 0% -> 0%
where the time goes in v2:
time: 95 us; the launch traced here: 93.8 us
  Pallas kernels  89.5 us (94%)
  local copies, waits for them, and re-layouts  3.7 us (4%)
    pallas_call x1, Pallas kernels, body(): pl.pallas_call(kernel, out_shape=[jax.ShapeDtypeStruct((frames, heads, po...  89.5 us
    unnamed x7, local copies, waits for them, and re-layouts  3.7 us

profile of v2, /device:TPU:1, one launch (start us, length us, event | category | flops | bytes accessed | tf_op | source)
XLA Modules:
  0.0 93.8 jit_solution(8029926610723790209)
XLA Ops:
  0.6 89.5 %shard_map.76 = (bf16[4,12,32,128]{3,2,1,0:T(8,128)(2,1)}, bf16[4,12,32,128]{3,2,1,0:T(8,128)(2,1)}, bf16[4,12,32,128]{3,2,1,0:T(8,128)(2,1)}) custom-call(bf16[4,12,32,128]{3,2,1,0:T(8,128)(2,1)} %bitcast.6, bf16[4,12,32,128]{3,2,1,0:T(8,128)(2,1)} %bitcast.7, bf16[4,12,32,128]{3,2,1,0:T(8,128)(2,1)} %bitcast.8, bf16[4,32,3072]{2,1,0:T(8,128)(2,1)} %x_ref.1, ...), custom_call_target="tpu_custom_call" | custom-call | tf_op jit(solution)/shard_map/pallas_call | solution.py:318
  90.1 0.0 copy-start.1
  90.1 1.8 %copy.11 = bf16[4,32,12,128]{3,1,2,0:T(8,128)(2,1)} copy(bf16[4,32,12,128]{3,1,2,0:T(8,128)(2,1)} %bitcast.11) | data formatting | bytes 786432
  91.9 0.0 copy-done.1
  91.9 0.0 copy-start
  91.9 0.7 copy.12
  92.7 0.4 copy-done
  93.1 0.7 copy.13
Async XLA Ops:
  90.1 1.8 %copy-start.1 = (bf16[4,12,32,128]{3,2,1,0:T(8,128)(2,1)S(1)}, bf16[4,12,32,128]{3,2,1,0:T(8,128)(2,1)}, u32[]{:S(2)}) copy-start(bf16[4,12,32,128]{3,2,1,0:T(8,128)(2,1)} %get-tuple-element.7) | copy-start | bytes 1179652
  91.9 1.1 %copy-start = (bf16[4,12,32,128]{3,2,1,0:T(8,128)(2,1)S(1)}, bf16[4,12,32,128]{3,2,1,0:T(8,128)(2,1)}, u32[]{:S(2)}) copy-start(bf16[4,12,32,128]{3,2,1,0:T(8,128)(2,1)} %get-tuple-element.8) | copy-start | bytes 1179652

commit v3 on v2

--- a/solution.py
+++ b/solution.py
@@ -21,7 +21,7 @@
 
 
 def kernel(q_ref, k_ref, v_ref, x_ref, w_ref, dq_ref, dk_ref, dv_ref,
-           qin, wbuf, xbuf, snd, rcv, gst_a, gs_a, gr_a, os_a, or_a, gst_b, gs_b, gr_b, os_b, or_b, out,
+           qin, wbuf, xbuf, snd, rcv, gst_a, gs_a, gr_a, os_a, or_a, out,
            in_sem, w_send, sib_send, sib_recv, e_recv, x_send, x_recv, xh_recv,
            gx_send, gx_recv, out_sem, qkv_s, qkv_r, g_s, g_r, o_s, o_r):
     t = lax.axis_index("tm")
@@ -50,7 +50,10 @@
     inner = (jnp.where(yl == 0, 1, NYL - 2) * NZ + z, f)
 
     def peer(d):
-        return ((yl + d // NZ) % NYL) * NZ + (z + 5 * (d % NZ)) % NZ
+        away = d - NZ
+        dy = jnp.where(d < NZ, 0, 1 + away % (NYL - 1))
+        dz = jnp.where(d < NZ, 5 * d, 5 * (away // (NYL - 1)))
+        return ((yl + dy) % NYL) * NZ + (z + dz) % NZ
 
     def block(yy, cc, i=0, n=NE):
         start = pl.multiple_of((yy * NC + cc) * wrows + i * part, 8)
@@ -83,10 +86,14 @@
     for cp in loads[:3]:
         cp.wait()
 
-    @pl.loop(0, heads)
-    def _(h):
-        for i in range(3):
-            snd_v[i, h] = mm(to_pos, qin[i, :, h].reshape(rows, size), 1, 0).astype(BF16)
+    order = (x, right, left, far)
+
+    @pl.loop(0, group)
+    def _(j):
+        for r in range(NX):
+            for i in range(3):
+                src = qin[i, :, order[r] * group + j].reshape(rows, size)
+                snd_v[i, r * group + j] = mm(to_pos, src, 1, 0).astype(BF16)
 
     pl.semaphore_wait(barrier, NT - 1 + len(others))
 
@@ -127,17 +134,34 @@
     send(x_ref, xbuf.at[x], x_send.at[1], x_recv.at[1], along_x(left))
     send(w_ref, block(yh, c), sib_send.at[NE], sib_recv.at[NE], sib)
 
-    pltpu.make_async_copy(snd.at[:, :, t], rcv.at[:, :, t], qkv_r).start()
-
-    @pl.loop(1, NT)
-    def _(d):
-        p = peer(d)
-        rcopy(snd.at[:, :, p], rcv.at[:, :, t], qkv_s, qkv_r, (p, f)).start()
-
-    order = (x, right, left, far)
-    first = (group - 1) * yh
-    rest = 1 - yh
-    nb = group - 1
+    parts = (pl.ds(0, group), pl.ds(group, heads - group))
+    for i, hs in enumerate(parts):
+        pltpu.make_async_copy(snd.at[:, hs, t], rcv.at[:, hs, t], qkv_r.at[i]).start()
+
+    def send_qkv(i, lo, hi):
+        hs = parts[i]
+
+        @pl.loop(lo, hi)
+        def _(d):
+            p = peer(d)
+            rcopy(snd.at[:, hs, p], rcv.at[:, hs, t], qkv_s.at[i], qkv_r.at[i], (p, f)).start()
+
+    for i in range(2):
+        send_qkv(i, 1, NZ)
+
+    @pl.when(edge)
+    def _():
+        for i in range(NE):
+            arrived(block(oh, c, i, 1), e_recv.at[i])
+            to_inner[i].start()
+            to_sib[i].start()
+
+    send_qkv(0, NZ, NT)
+
+    @pl.when(jnp.logical_not(edge))
+    def _():
+        send_qkv(1, NZ, NT)
+
 
     class Phase:
         def __init__(self, gst, gs, gr, os, orr, count, head, sems):
@@ -150,12 +174,10 @@
             self.orr_v = orr.reshape(3, n, rows, size)
             self.count, self.head, self.sems = count, head, sems
 
-    pa = Phase(gst_a, gs_a, gr_a, os_a, or_a, 1, first, 0)
-    pb = Phase(gst_b, gs_b, gr_b, os_b, or_b, nb, rest, 3)
+    pa = Phase(gst_a, gs_a, gr_a, os_a, or_a, group, 0, 0)
 
     def project(ph, xx):
-        ws = pl.ds(pl.multiple_of(ph.head * size, size), ph.count * size)
-        acc = mm(xbuf[xx].reshape(rows, -1), wbuf[ws, :], 1, 1).astype(BF16)
+        acc = mm(xbuf[xx].reshape(rows, -1), wbuf[...], 1, 1).astype(BF16)
         return mm(to_pos, acc, 1, 0).astype(BF16)
 
     def own_g(ph):
@@ -194,7 +216,7 @@
         arrived(ph.gr.at[hs], g_r.at[step])
         for i in range(lo, lo + n):
             for j in range(ph.count):
-                h, m = order[i] * group + ph.head + j, i * ph.count + j
+                h = m = i * ph.count + j
                 q, k, v, g = rcv_v[0, h], rcv_v[1, h], rcv_v[2, h], ph.gr_v[m]
                 s = mm(k, q, 1, 1) * scale
                 e = jnp.exp(s - jnp.max(s, axis=0, keepdims=True))
@@ -229,16 +251,10 @@
                 cp.start()
                 stores.append(cp)
 
-    loads[3].wait()
-    loads[4].wait()
-    arrived(block(yh, 1 - c), sib_recv.at[NE])
-    own_g(pa)
-
-    @pl.when(edge)
+    @pl.when(jnp.logical_not(edge))
     def _():
         for i in range(NE):
             arrived(block(oh, c, i, 1), e_recv.at[i])
-            to_inner[i].start()
             to_sib[i].start()
 
     hf = frames // 2
@@ -248,36 +264,34 @@
     arrived(xbuf.at[right], x_recv.at[1])
     high = xbuf.at[right, pl.ds(hf, hf)]
     send(high, high, x_send.at[3], xh_recv.at[1], along_x(left))
+
+    loads[3].wait()
+    loads[4].wait()
+    arrived(block(yh, 1 - c), sib_recv.at[NE])
+    for i in range(NE):
+        arrived(block(oh, 1 - c, i, 1), sib_recv.at[i])
     return_g(pa, 0)
     return_g(pa, 1)
+    own_g(pa)
+    send_g(pa, 0, 1)
+
+    @pl.when(edge)
+    def _():
+        send_qkv(1, NZ, NT)
+
+    take_g(pa, 1)
+    take_g(pa, 2)
+    send_g(pa, 1, 2)
     arrived(xbuf.at[far, pl.ds(0, hf)], xh_recv.at[0])
     arrived(xbuf.at[far, pl.ds(hf, hf)], xh_recv.at[1])
     return_g(pa, 2)
-
-    @pl.when(jnp.logical_not(edge))
-    def _():
-        for i in range(NE):
-            arrived(block(oh, c, i, 1), e_recv.at[i])
-            to_sib[i].start()
-
-    for slot in (1, 2, 3):
-        take_g(pa, slot)
-    send_g(pa, 0, 4)
-
-    for i in range(NE):
-        arrived(block(oh, 1 - c, i, 1), sib_recv.at[i])
-    for i in range(3):
-        return_g(pb, i)
-    own_g(pb)
-    take_g(pb, 1)
-    send_g(pb, 0, 2)
-    take_g(pb, 2)
-    take_g(pb, 3)
-    send_g(pb, 2, 2)
-
-    arrived(rcv, qkv_r)
-    for step in range(3):
-        attend(step)
+    take_g(pa, 3)
+    send_g(pa, 3, 1)
+    arrived(rcv.at[:, parts[0]], qkv_r.at[0])
+    attend(0)
+    arrived(rcv.at[:, parts[1]], qkv_r.at[1])
+    attend(1)
+    attend(2)
     for step in range(3):
         finish(step)
     for cp in stores:
@@ -291,13 +305,29 @@
         for cp in to_mirror + to_inner:
             cp.wait_send()
 
-    others = snd.at[:, :, pl.ds(0, NT - 1)]
-    pltpu.make_async_copy(others, others, qkv_s).wait()
+    for i, hs in enumerate(parts):
+        others = snd.at[:, hs, pl.ds(0, NT - 1)]
+        pltpu.make_async_copy(others, others, qkv_s.at[i]).wait()
     for step, (ph, lo, n, hs) in enumerate(steps):
         others = ph.gs.at[hs, pl.ds(0, NT - 1)]
         pltpu.make_async_copy(others, others, g_s.at[step]).wait()
         others = ph.os.at[:, hs, pl.ds(0, NT - 1)]
         pltpu.make_async_copy(others, others, o_s.at[step]).wait()
+
+
+def copy_out(a_ref, b_ref, c_ref, x_ref, y_ref, z_ref, buf, in_sem, out_sem):
+    frames = a_ref.shape[0]
+    pairs = ((a_ref, x_ref), (b_ref, y_ref), (c_ref, z_ref))
+    pieces = [(j, i) for j in range(3) for i in range(frames)]
+    loads = [pltpu.make_async_copy(pairs[j][0].at[i], buf.at[j, i], in_sem.at[j * frames + i]) for j, i in pieces]
+    stores = [pltpu.make_async_copy(buf.at[j, i], pairs[j][1].at[i], out_sem.at[j * frames + i]) for j, i in pieces]
+    for cp in loads:
+        cp.start()
+    for load, store in zip(loads, stores):
+        load.wait()
+        store.start()
+    for cp in stores:
+        cp.wait()
 
 
 def body(queries, key_states, value_states, out_grad, out_proj):
@@ -326,16 +356,23 @@
             pltpu.VMEM((NX, frames, pos, width), BF16),
             pltpu.VMEM((3, heads, pos, frames, size), BF16),
             pltpu.VMEM((3, heads, NT, frames, size), BF16),
-            *phase(1),
-            *phase(heads // NX - 1),
+            *phase(heads // NX),
             pltpu.VMEM((3, frames, heads, pos, size), BF16),
             dma((5,)), dma((2 * NE,)), dma((NE + 1,)), dma((NE + 1,)), dma((NE,)),
-            dma((4,)), dma((2,)), dma((2,)), dma((6,)), dma((6,)), dma((3 * heads,)),
-            dma, dma, dma((3,)), dma((3,)), dma((3,)), dma((3,)),
+            dma((4,)), dma((2,)), dma((2,)), dma((3,)), dma((3,)), dma((3 * NX,)),
+            dma((2,)), dma((2,)), dma((3,)), dma((3,)), dma((3,)), dma((3,)),
         ],
         compiler_params=pltpu.CompilerParams(
             collective_id=0, has_side_effects=True, vmem_limit_bytes=60 << 20),
     )(turn(queries), turn(key_states), turn(value_states), out_grad, out_proj)
+    outs = pl.pallas_call(
+        copy_out,
+        out_shape=[jax.ShapeDtypeStruct((frames, heads, pos, size), BF16)] * 3,
+        in_specs=[hbm] * 3,
+        out_specs=[hbm] * 3,
+        scratch_shapes=[pltpu.VMEM((3, frames, heads, pos, size), BF16), dma((3 * frames,)), dma((3 * frames,))],
+        compiler_params=pltpu.CompilerParams(vmem_limit_bytes=60 << 20),
+    )(*outs)
     return tuple(turn(o) for o in outs)
 
 

time: 95 us -> 90.9 us (0.957)
  the two profiles are of different devices: /device:TPU:1 before, /device:TPU:9 now
where the time goes in v3:
time: 90.9 us; the launch traced here: 90.7 us
  Pallas kernels  90.1 us (99%)
    pallas_call x1, Pallas kernels, body(): pl.pallas_call(kernel, out_shape=[jax.ShapeDtypeStruct((frames, heads, po...  87.9 us
    pallas_call x1, Pallas kernels, body(): pl.pallas_call(copy_out, out_shape=[jax.ShapeDtypeStruct((frames, heads,...  2.2 us

profile of v3, /device:TPU:9, one launch (start us, length us, event | category | flops | bytes accessed | tf_op | source)
XLA Modules:
  0.0 90.7 jit_solution(17004086013814546144)
XLA Ops:
  0.6 87.9 %shard_map.76 = (bf16[4,12,32,128]{3,2,1,0:T(8,128)(2,1)}, bf16[4,12,32,128]{3,2,1,0:T(8,128)(2,1)}, bf16[4,12,32,128]{3,2,1,0:T(8,128)(2,1)}) custom-call(bf16[4,12,32,128]{3,2,1,0:T(8,128)(2,1)} %bitcast.6, bf16[4,12,32,128]{3,2,1,0:T(8,128)(2,1)} %bitcast.7, bf16[4,12,32,128]{3,2,1,0:T(8,128)(2,1)} %bitcast.8, bf16[4,32,3072]{2,1,0:T(8,128)(2,1)} %x_ref.1, ...), custom_call_target="tpu_custom_call" | custom-call | tf_op jit(solution)/shard_map/pallas_call | solution.py:348
  88.5 2.2 %shard_map.77 = (bf16[4,12,32,128]{3,2,1,0:T(8,128)(2,1)}, bf16[4,12,32,128]{3,2,1,0:T(8,128)(2,1)}, bf16[4,12,32,128]{3,2,1,0:T(8,128)(2,1)}) custom-call(bf16[4,12,32,128]{3,2,1,0:T(8,128)(2,1)} %get-tuple-element.9.a_ref, bf16[4,12,32,128]{3,2,1,0:T(8,128)(2,1)} %get-tuple-element.10.b_ref, bf16[4,12,32,128]{3,2,1,0:T(8,128)(2,1)} %get-tuple-element.11.c_ref), custom_call_target="tpu_custom_call" | custom-call | tf_op jit(solution)/shard_map/pallas_call | solution.py:368

commit v4 on v3

--- a/solution.py
+++ b/solution.py
@@ -21,9 +21,9 @@
 
 
 def kernel(q_ref, k_ref, v_ref, x_ref, w_ref, dq_ref, dk_ref, dv_ref,
-           qin, wbuf, xbuf, snd, rcv, gst_a, gs_a, gr_a, os_a, or_a, out,
+           qin, wbuf, xbuf, snd, rcv, gst_a, gs_a, gr_a, os_a, or_a,
            in_sem, w_send, sib_send, sib_recv, e_recv, x_send, x_recv, xh_recv,
-           gx_send, gx_recv, out_sem, qkv_s, qkv_r, g_s, g_r, o_s, o_r):
+           gx_send, gx_recv, qkv_s, qkv_r, g_s, g_r, o_s, o_r):
     t = lax.axis_index("tm")
     f = lax.axis_index("fsdp")
     yl, z = t // NZ, t % NZ
@@ -88,12 +88,15 @@
 
     order = (x, right, left, far)
 
-    @pl.loop(0, group)
-    def _(j):
-        for r in range(NX):
-            for i in range(3):
-                src = qin[i, :, order[r] * group + j].reshape(rows, size)
-                snd_v[i, r * group + j] = mm(to_pos, src, 1, 0).astype(BF16)
+    def permute(xs):
+        @pl.loop(0, group)
+        def _(j):
+            for r in xs:
+                for i in range(3):
+                    src = qin[i, :, order[r] * group + j].reshape(rows, size)
+                    snd_v[i, r * group + j] = mm(to_pos, src, 1, 0).astype(BF16)
+
+    permute((0,))
 
     pl.semaphore_wait(barrier, NT - 1 + len(others))
 
@@ -135,7 +138,8 @@
     send(w_ref, block(yh, c), sib_send.at[NE], sib_recv.at[NE], sib)
 
     parts = (pl.ds(0, group), pl.ds(group, heads - group))
-    for i, hs in enumerate(parts):
+    def keep_qkv(i):
+        hs = parts[i]
         pltpu.make_async_copy(snd.at[:, hs, t], rcv.at[:, hs, t], qkv_r.at[i]).start()
 
     def send_qkv(i, lo, hi):
@@ -146,8 +150,16 @@
             p = peer(d)
             rcopy(snd.at[:, hs, p], rcv.at[:, hs, t], qkv_s.at[i], qkv_r.at[i], (p, f)).start()
 
-    for i in range(2):
-        send_qkv(i, 1, NZ)
+    keep_qkv(0)
+    send_qkv(0, 1, NZ)
+
+    @pl.when(jnp.logical_not(edge))
+    def _():
+        send_qkv(0, NZ, NT)
+
+    permute((1, 2, 3))
+    keep_qkv(1)
+    send_qkv(1, 1, NZ)
 
     @pl.when(edge)
     def _():
@@ -156,7 +168,7 @@
             to_inner[i].start()
             to_sib[i].start()
 
-    send_qkv(0, NZ, NT)
+        send_qkv(0, NZ, NT)
 
     @pl.when(jnp.logical_not(edge))
     def _():
@@ -235,21 +247,14 @@
             p = peer(d)
             rcopy(ph.os.at[:, hs, p], ph.orr.at[:, hs, t], o_s.at[step], o_r.at[step], (p, f)).start()
 
-    stores = []
-
     def finish(step):
         ph, lo, n, hs = steps[step]
         arrived(ph.orr.at[:, hs], o_r.at[step])
         for j, ref in enumerate((dq_ref, dk_ref, dv_ref)):
             for i in range(lo, lo + n):
-                start = order[i] * group + ph.head
                 for u in range(ph.count):
-                    out[j, :, start + u] = mm(to_frame, ph.orr_v[j, i * ph.count + u], 1, 0).astype(BF16).reshape(
-                        frames, pos, size)
-                cp = pltpu.make_async_copy(out.at[j, :, pl.ds(start, ph.count)], ref.at[:, pl.ds(start, ph.count)],
-                                           out_sem.at[len(stores)])
-                cp.start()
-                stores.append(cp)
+                    ref[:, order[i] * group + ph.head + u] = mm(
+                        to_frame, ph.orr_v[j, i * ph.count + u], 1, 0).astype(BF16).reshape(frames, pos, size)
 
     @pl.when(jnp.logical_not(edge))
     def _():
@@ -294,9 +299,6 @@
     attend(2)
     for step in range(3):
         finish(step)
-    for cp in stores:
-        cp.wait()
-
     for cp in sent + to_sib:
         cp.wait_send()
 
@@ -315,18 +317,16 @@
         pltpu.make_async_copy(others, others, o_s.at[step]).wait()
 
 
-def copy_out(a_ref, b_ref, c_ref, x_ref, y_ref, z_ref, buf, in_sem, out_sem):
+def copy_out(a_ref, b_ref, c_ref, x_ref, y_ref, z_ref, sem):
     frames = a_ref.shape[0]
-    pairs = ((a_ref, x_ref), (b_ref, y_ref), (c_ref, z_ref))
-    pieces = [(j, i) for j in range(3) for i in range(frames)]
-    loads = [pltpu.make_async_copy(pairs[j][0].at[i], buf.at[j, i], in_sem.at[j * frames + i]) for j, i in pieces]
-    stores = [pltpu.make_async_copy(buf.at[j, i], pairs[j][1].at[i], out_sem.at[j * frames + i]) for j, i in pieces]
-    for cp in loads:
+    copies = [
+        pltpu.make_async_copy(src.at[i], dst.at[i], sem.at[j * frames + i])
+        for j, (src, dst) in enumerate(((a_ref, x_ref), (b_ref, y_ref), (c_ref, z_ref)))
+        for i in range(frames)
+    ]
+    for cp in copies:
         cp.start()
-    for load, store in zip(loads, stores):
-        load.wait()
-        store.start()
-    for cp in stores:
+    for cp in copies:
         cp.wait()
 
 
@@ -334,6 +334,7 @@
     frames, pos, heads, size = queries.shape
     wrows, width = out_proj.shape
     hbm = pl.BlockSpec(memory_space=pltpu.HBM)
+    vmem = pl.BlockSpec(memory_space=pltpu.VMEM)
     dma = pltpu.SemaphoreType.DMA
 
     def turn(a):
@@ -349,7 +350,7 @@
         kernel,
         out_shape=[jax.ShapeDtypeStruct((frames, heads, pos, size), BF16)] * 3,
         in_specs=[hbm] * 5,
-        out_specs=[hbm] * 3,
+        out_specs=[vmem] * 3,
         scratch_shapes=[
             pltpu.VMEM((3, frames, heads, pos, size), BF16),
             pltpu.VMEM((NYH * NC * wrows, width), BF16),
@@ -357,21 +358,21 @@
             pltpu.VMEM((3, heads, pos, frames, size), BF16),
             pltpu.VMEM((3, heads, NT, frames, size), BF16),
             *phase(heads // NX),
-            pltpu.VMEM((3, frames, heads, pos, size), BF16),
             dma((5,)), dma((2 * NE,)), dma((NE + 1,)), dma((NE + 1,)), dma((NE,)),
-            dma((4,)), dma((2,)), dma((2,)), dma((3,)), dma((3,)), dma((3 * NX,)),
+            dma((4,)), dma((2,)), dma((2,)), dma((3,)), dma((3,)),
             dma((2,)), dma((2,)), dma((3,)), dma((3,)), dma((3,)), dma((3,)),
         ],
         compiler_params=pltpu.CompilerParams(
-            collective_id=0, has_side_effects=True, vmem_limit_bytes=60 << 20),
-    )(turn(queries), turn(key_states), turn(value_states), out_grad, out_proj)
+            collective_id=0, has_side_effects=True, vmem_limit_bytes=40 << 20),
+    )(*[pltpu.with_memory_space_constraint(a, pltpu.HBM)
+        for a in (turn(queries), turn(key_states), turn(value_states), out_grad, out_proj)])
     outs = pl.pallas_call(
         copy_out,
         out_shape=[jax.ShapeDtypeStruct((frames, heads, pos, size), BF16)] * 3,
-        in_specs=[hbm] * 3,
+        in_specs=[vmem] * 3,
         out_specs=[hbm] * 3,
-        scratch_shapes=[pltpu.VMEM((3, frames, heads, pos, size), BF16), dma((3 * frames,)), dma((3 * frames,))],
-        compiler_params=pltpu.CompilerParams(vmem_limit_bytes=60 << 20),
+        scratch_shapes=[dma((3 * frames,))],
+        compiler_params=pltpu.CompilerParams(vmem_limit_bytes=40 << 20),
     )(*outs)
     return tuple(turn(o) for o in outs)
 

time: 90.9 us -> 89 us (0.979)
  Pallas kernels: 90.1 us -> 88.2 us
    pallas_call x1, Pallas kernels: 2.2 us -> 1.1 us  [body(): pl.pallas_call(copy_out, out_shape=[jax.ShapeDtypeStruct((frames, heads,...]
where the time goes in v4:
time: 89 us; the launch traced here: 88.9 us
  Pallas kernels  88.2 us (99%)
    pallas_call x1, Pallas kernels, body(): pl.pallas_call(kernel, out_shape=[jax.ShapeDtypeStruct((frames, heads, po...  87.1 us

profile of v4, /device:TPU:9, one launch (start us, length us, event | category | flops | bytes accessed | tf_op | source)
XLA Modules:
  0.0 88.9 jit_solution(1323614884403907064)
XLA Ops:
  0.6 87.1 %shard_map.76 = (bf16[4,12,32,128]{3,2,1,0:T(8,128)(2,1)S(1)}, bf16[4,12,32,128]{3,2,1,0:T(8,128)(2,1)S(1)}, bf16[4,12,32,128]{3,2,1,0:T(8,128)(2,1)S(1)}) custom-call(bf16[4,12,32,128]{3,2,1,0:T(8,128)(2,1)} %bitcast.6, bf16[4,12,32,128]{3,2,1,0:T(8,128)(2,1)} %bitcast.7, bf16[4,12,32,128]{3,2,1,0:T(8,128)(2,1)} %bitcast.8, bf16[4,32,3072]{2,1,0:T(8,128)(2,1)} %x_ref.1, ...), custom_call_target="tpu_custom_call" | custom-call | tf_op jit(solution)/shard_map/pallas_call | solution.py:349
  87.8 1.1 %shard_map.77 = (bf16[4,12,32,128]{3,2,1,0:T(8,128)(2,1)}, bf16[4,12,32,128]{3,2,1,0:T(8,128)(2,1)}, bf16[4,12,32,128]{3,2,1,0:T(8,128)(2,1)}) custom-call(bf16[4,12,32,128]{3,2,1,0:T(8,128)(2,1)S(1)} %get-tuple-element.9.a_ref, bf16[4,12,32,128]{3,2,1,0:T(8,128)(2,1)S(1)} %get-tuple-element.10.b_ref, bf16[4,12,32,128]{3,2,1,0:T(8,128)(2,1)S(1)} %get-tuple-element.11.c_ref), custom_call_target="tpu_custom_call" | custom-call | tf_op jit(solution)/shard_map/pallas_call | solution.py:369

commit v5 on v4

--- a/solution.py
+++ b/solution.py
@@ -96,7 +96,7 @@
                     src = qin[i, :, order[r] * group + j].reshape(rows, size)
                     snd_v[i, r * group + j] = mm(to_pos, src, 1, 0).astype(BF16)
 
-    permute((0,))
+    permute((0, 1))
 
     pl.semaphore_wait(barrier, NT - 1 + len(others))
 
@@ -137,7 +137,7 @@
     send(x_ref, xbuf.at[x], x_send.at[1], x_recv.at[1], along_x(left))
     send(w_ref, block(yh, c), sib_send.at[NE], sib_recv.at[NE], sib)
 
-    parts = (pl.ds(0, group), pl.ds(group, heads - group))
+    parts = (pl.ds(0, 2 * group), pl.ds(2 * group, heads - 2 * group))
     def keep_qkv(i):
         hs = parts[i]
         pltpu.make_async_copy(snd.at[:, hs, t], rcv.at[:, hs, t], qkv_r.at[i]).start()
@@ -157,7 +157,7 @@
     def _():
         send_qkv(0, NZ, NT)
 
-    permute((1, 2, 3))
+    permute((2, 3))
     keep_qkv(1)
     send_qkv(1, 1, NZ)
 

time: 89 us -> 88.4 us (level)
  the two profiles are of different devices: /device:TPU:9 before, /device:TPU:1 now
where the time goes in v5:
time: 88.4 us; the launch traced here: 86.8 us
  Pallas kernels  86.1 us (97%)
    pallas_call x1, Pallas kernels, body(): pl.pallas_call(kernel, out_shape=[jax.ShapeDtypeStruct((frames, heads, po...  85 us

profile of v5, /device:TPU:1, one launch (start us, length us, event | category | flops | bytes accessed | tf_op | source)
XLA Modules:
  0.0 86.8 jit_solution(13443103089934254997)
XLA Ops:
  0.6 85.0 %shard_map.76 = (bf16[4,12,32,128]{3,2,1,0:T(8,128)(2,1)S(1)}, bf16[4,12,32,128]{3,2,1,0:T(8,128)(2,1)S(1)}, bf16[4,12,32,128]{3,2,1,0:T(8,128)(2,1)S(1)}) custom-call(bf16[4,12,32,128]{3,2,1,0:T(8,128)(2,1)} %bitcast.6, bf16[4,12,32,128]{3,2,1,0:T(8,128)(2,1)} %bitcast.7, bf16[4,12,32,128]{3,2,1,0:T(8,128)(2,1)} %bitcast.8, bf16[4,32,3072]{2,1,0:T(8,128)(2,1)} %x_ref.1, ...), custom_call_target="tpu_custom_call" | custom-call | tf_op jit(solution)/shard_map/pallas_call | solution.py:349
  85.7 1.1 %shard_map.77 = (bf16[4,12,32,128]{3,2,1,0:T(8,128)(2,1)}, bf16[4,12,32,128]{3,2,1,0:T(8,128)(2,1)}, bf16[4,12,32,128]{3,2,1,0:T(8,128)(2,1)}) custom-call(bf16[4,12,32,128]{3,2,1,0:T(8,128)(2,1)S(1)} %get-tuple-element.9.a_ref, bf16[4,12,32,128]{3,2,1,0:T(8,128)(2,1)S(1)} %get-tuple-element.10.b_ref, bf16[4,12,32,128]{3,2,1,0:T(8,128)(2,1)S(1)} %get-tuple-element.11.c_ref), custom_call_target="tpu_custom_call" | custom-call | tf_op jit(solution)/shard_map/pallas_call | solution.py:369
